TPU v7x, 256 devices: a whole 4x4x8 slice. The times are simulated.
256 devices in a mesh: narrow: 8 (over y, z_lo), wide: 8 (over z_hi, core), nys: 4 (over x).
Axes of the slice: x: 4, y: 4, z: 8 (z_hi: 4, z_lo: 2; z = z_hi * 2 + z_lo), core: 2. Of those that a mesh axis runs over, the one named last changes fastest.
Arguments:
- centers: bfloat16 [262144, 1024], P(('narrow', 'wide', 'nys')), may hold values from -6 to 6
- weights: float32 [262144, 1000], P(('narrow', 'wide', 'nys')), may hold values from -6 to 6
- batch_points: bfloat16 [512, 1024], P(('narrow', 'wide', 'nys')), may hold values from -6 to 6
- labels: float32 [512, 1000], P(('narrow', 'wide', 'nys')), may hold values from -6 to 6
- nystrom_points: bfloat16 [2048, 1024], P(('narrow', 'nys')), may hold values from -6 to 6
- eigvecs: float32 [2048, 160], P(('narrow', 'nys')), may hold values from -0.125 to 0.125
- corrections: float32 [160], replicated, may hold values from 0.05 to 0.5
Outputs:
- new_weights: float32 [262144, 1000], P(('narrow', 'wide', 'nys'))
All inputs are finite; a program needn't handle non-finite values.
Results may differ from a plain program's by a relative error of at most 0.0003.
The roundings to bfloat16 on the way count: a program that leaves them out, or rounds other values in their place, can miss the bound.
Values may be sent and summed in bfloat16 or wider, within the bound.
A program may use at most 64 MiB of HBM per device.

v0:
```python
import math
import jax
import jax.numpy as jnp
from jax import lax
from jax.sharding import PartitionSpec as P

BATCH = 512
RATE = 16.0
SPREAD = 4.0


def kernel_with(left, left_sq, right):
    cross = lax.dot_general(
        left, right, (((1,), (1,)), ((), ())), preferred_element_type=jnp.float32
    )
    right_sq = jnp.sum(jnp.square(right.astype(jnp.float32)), axis=1)
    dist = jnp.sqrt(jnp.maximum(left_sq[:, None] + right_sq[None, :] - 2.0 * cross, 0.0))
    radius = math.sqrt(2.0 * left.shape[1])
    return jnp.exp((radius - dist) / SPREAD).astype(jnp.bfloat16)


def squares(points):
    return jnp.sum(jnp.square(points.astype(jnp.float32)), axis=1)


def per_device(centers, weights, batch_points, labels, nystrom_points, eigvecs, corrections):
    batch_all = lax.all_gather(batch_points, ("narrow", "wide", "nys"), axis=0, tiled=True)
    count = lax.axis_size(("narrow", "wide", "nys"))
    scale = (centers.shape[0] * count) ** (-0.5)
    center_sq = squares(centers)
    k_batch = kernel_with(centers, center_sq, batch_all)
    partial_value = (
        lax.dot_general(
            k_batch,
            weights.astype(jnp.bfloat16),
            (((0,), (0,)), ((), ())),
            preferred_element_type=jnp.float32,
        )
        * scale
    )
    rows = labels.shape[0]
    offset = lax.axis_index(("narrow", "wide", "nys")) * rows
    placed = lax.dynamic_update_slice(jnp.zeros_like(partial_value), labels, (offset, jnp.int32(0)))
    residual = lax.psum(partial_value - placed, ("narrow", "wide", "nys")).astype(jnp.bfloat16)
    k_nystrom = kernel_with(nystrom_points, squares(nystrom_points), batch_all)
    pulled = jnp.dot(k_nystrom, residual, preferred_element_type=jnp.float32)
    local_proj = lax.dot_general(
        eigvecs, pulled, (((0,), (0,)), ((), ())), precision=lax.Precision.HIGHEST
    )
    projected = lax.psum(local_proj, ("narrow", "nys"))
    scaled_proj = corrections[:, None] * projected
    gradient = jnp.dot(k_batch, residual, preferred_element_type=jnp.float32)
    corrected = jnp.dot(eigvecs, scaled_proj, precision=lax.Precision.HIGHEST).astype(jnp.bfloat16)
    points = lax.all_gather(nystrom_points, ("narrow", "nys"), axis=0, tiled=True)
    coefs = lax.all_gather(corrected, ("narrow", "nys"), axis=0, tiled=True)
    tile = kernel_with(centers, center_sq, points)
    nystrom_term = jnp.dot(tile, coefs, preferred_element_type=jnp.float32)
    return weights - RATE / BATCH * (gradient - nystrom_term)


def solution(mesh):
    placed = (
        P(("narrow", "wide", "nys"), None),
        P(("narrow", "wide", "nys"), None),
        P(("narrow", "wide", "nys"), None),
        P(("narrow", "wide", "nys"), None),
        P(("narrow", "nys"), None),
        P(("narrow", "nys"), None),
        P(),
    )
    return jax.shard_map(
        per_device,
        mesh=mesh,
        in_specs=placed,
        out_specs=P(("narrow", "wide", "nys"), None),
        check_vma=False,
    )
```

profile of v0, /device:TPU:2, one launch (start us, length us, event | category | flops | bytes accessed | tf_op | source)
XLA Modules:
  0.0 1286.6 jit_solution(18334620316952581570)
XLA Ops:
  6.5 0.0 copy-start
  6.5 0.0 all-gather.9.cloned.1.call-start
  6.5 0.7 all-gather.9.cloned.1.call-update
  7.3 0.0 all-reduce.3.cloned.1.call-start
  7.3 0.9 copy.9
  8.2 0.2 broadcast_in_dim.2
  8.5 6.3 dynamic_update_slice.3
  14.8 1.0 multiply_reduce_fusion.3
  15.8 2.1 multiply_reduce_fusion.1
  17.9 523.6 %all-gather.9.cloned.1.call-done = bf16[256,2,1024]{2,1,0:T(2,128)(2,1)} async-done(((bf16[1,2,1024]{2,1,0:T(2,128)(2,1)}), bf16[256,2,1024]{2,1,0:T(2,128)(2,1)}) %all-gather.9.cloned.1.call-update) | async-done | bytes 1048592 | tf_op jit(solution)/shard_map/all_gather | solution.py:27
  541.5 1.5 reshape.6
  543.0 0.3 multiply_reduce_fusion.2
  543.3 0.0 copy-start.1
  543.3 3.8 exponential_convert_fusion.1
  547.1 0.0 copy-start.2
  547.1 1.1 copy-done.2
  548.2 0.0 copy-done.1
  548.2 0.0 copy-start.4
  548.2 2.6 multiply_subtract_fusion.1
  550.7 0.0 copy-start.5
  550.7 81.6 %all-reduce.4 = bf16[512,1000]{0,1:T(8,128)(2,1)S(1)} all-reduce(f32[512,1000]{0,1:T(8,128)} %multiply_subtract_fusion.1), channel_id=1, replica_groups=mesh['narrow'=8,'wide'=8,'nys'=4] {'narrow','wide','nys'}, use_global_device_ids=true, to_apply=%region_2.0 | all-reduce | flops 512000 | bytes 3072000 | tf_op jit(solution)/shard_map/psum | solution.py:44
  632.3 0.0 copy-done.4
  632.3 0.8 fusion.12
  633.2 0.0 copy-done
  633.2 1.6 convolution_bitcast_fusion
  634.7 0.0 all-reduce.3.cloned.1.call-update
  634.7 0.0 all-gather.5.cloned.1.call-start
  634.8 0.7 all-gather.5.cloned.1.call-update
  635.5 0.2 all-gather.7.cloned.1.call-start
  635.7 301.3 %all-reduce.3.cloned.1.call-done = f32[160,1000]{1,0:T(8,128)} async-done(((f32[160,1000]{1,0:T(8,128)}), f32[160,1000]{1,0:T(8,128)}) %all-reduce.3.cloned.1.call-update) | async-done | bytes 640016 | tf_op jit(solution)/shard_map/psum | solution.py:50
  937.0 0.0 copy-done.5
  937.0 2.3 fusion.4
  939.4 0.0 all-gather.7.cloned.1.call-update
  939.4 157.5 %all-gather.5.cloned.1.call-done = bf16[2048,1024]{1,0:T(8,128)(2,1)} async-done(((bf16[64,1024]{1,0:T(8,128)(2,1)}), bf16[2048,1024]{1,0:T(8,128)(2,1)}) %all-gather.5.cloned.1.call-update) | async-done | bytes 4194320 | tf_op jit(solution)/shard_map/all_gather | solution.py:54
  1097.0 3.1 multiply_reduce_fusion
  1100.0 0.0 copy-start.3
  1100.1 157.9 %all-gather.7.cloned.1.call-done = bf16[2048,1000]{1,0:T(8,128)(2,1)} async-done(((bf16[64,1000]{1,0:T(8,128)(2,1)}), bf16[2048,1000]{1,0:T(8,128)(2,1)}) %all-gather.7.cloned.1.call-update) | async-done | bytes 4096016 | tf_op jit(solution)/shard_map/all_gather | solution.py:55
  1258.0 15.5 %fusion.13 = f32[1024,1000]{0,1:T(8,128)} fusion(bf16[2048,1000]{1,0:T(8,128)(2,1)} %all-gather.7.cloned.1.call-done, bf16[1024,1024]{1,0:T(8,128)(2,1)} %param.7, bf16[2048,1024]{1,0:T(8,128)(2,1)} %all-gather.5.cloned.1.call-done, f32[2048]{0:T(1024)S(1)} %multiply_reduce_fusion, f32[1024]{0:T(1024)S(1)} %multiply_reduce_fusion.1), kind=kOutput, calls=%fused_computation.21 | convolution fusion | flops 8503951360 | bytes 14495744 | tf_op jit(solution)/shard_map/dot_general | solution.py:57
  1273.5 0.0 copy-done.3
  1273.5 6.7 multiply_subtract_fusion
Async XLA Ops:
  6.5 626.6 %copy-start = (f32[64,160]{1,0:T(8,128)S(1)}, f32[64,160]{1,0:T(8,128)}, u32[]{:S(2)}) copy-start(f32[64,160]{1,0:T(8,128)} %param.12) | copy-start | bytes 122884
  6.5 535.0 %all-gather.9.cloned.1.call-start = ((), (), s32[]{:S(2)}) async-start(), calls=%async_computation.3 | async-start | bytes 1052672 | tf_op jit(solution)/shard_map/all_gather | solution.py:27
  7.3 929.8 %all-reduce.3.cloned.1.call-start = ((), (), s32[]{:S(2)}) async-start(), calls=%async_computation.1 | async-start | bytes 1310720 | tf_op jit(solution)/shard_map/psum | solution.py:50
  543.3 4.9 copy-start.1
  547.1 1.1 copy-start.2
  548.2 84.1 %copy-start.4 = (bf16[64,1024]{1,0:T(8,128)(2,1)S(1)}, bf16[64,1024]{1,0:T(8,128)(2,1)}, u32[]{:S(2)}) copy-start(bf16[64,1024]{1,0:T(8,128)(2,1)} %param.11) | copy-start | bytes 393220
  550.7 386.3 %copy-start.5 = (f32[160]{0:T(256)S(1)}, f32[160]{0:T(256)}, u32[]{:S(2)}) copy-start(f32[160]{0:T(256)} %param.13) | copy-start | bytes 1924
  634.7 462.2 %all-gather.5.cloned.1.call-start = ((), (), s32[]{:S(2)}) async-start(), calls=%async_computation | async-start | bytes 4325376 | tf_op jit(solution)/shard_map/all_gather | solution.py:54
  635.5 622.5 %all-gather.7.cloned.1.call-start = ((), (), s32[]{:S(2)}) async-start(), calls=%async_computation.2 | async-start | bytes 4325376 | tf_op jit(solution)/shard_map/all_gather | solution.py:55
  1100.0 173.4 %copy-start.3 = (bf16[1024,512]{1,0:T(8,128)(2,1)S(1)}, bf16[1024,512]{1,0:T(8,128)(2,1)}, u32[]{:S(2)}) copy-start(bf16[1024,512]{1,0:T(8,128)(2,1)} %copy-done.2) | copy-start | bytes 3145732
Sparse Core Ops, SparseCore 0:
  9.2 532.3 all-gather.8
  634.9 302.1 all-reduce.2
  939.0 157.9 all-gather.4
  1098.7 159.1 all-gather.6
where the time goes:
time: 1290 us
  waiting for transfers between devices  1140 us (88%)
  blocking collectives  81.6 us (6%)
  matrix products  33.3 us (3%)
  between operations  13.2 us (1%)
    all_gather x1, waiting for transfers between devices, per_device(): lax.all_gather(batch_points, ('narrow', 'wide', 'nys'), axis=0, tiled=True)  524 us
    psum x1, waiting for transfers between devices, per_device(): projected = lax.psum(local_proj, ('narrow', 'nys'))  301 us
    all_gather x1, waiting for transfers between devices, per_device(): coefs = lax.all_gather(corrected, ('narrow', 'nys'), axis=0, tiled=True)  158 us
    all_gather x1, waiting for transfers between devices, per_device(): lax.all_gather(nystrom_points, ('narrow', 'nys'), axis=0, tiled=True)  158 us
    psum x1, blocking collectives, per_device(): lax.psum(partial_value - placed, ('narrow', 'wide', 'nys'))  81.6 us
  transfers between devices with their start and end apart: 4, of which 4 were waited for; matrix products, arithmetic and copies ran while one was open for 1% of the time, Pallas kernels for 0%

commit v1 on v0

--- a/solution.py
+++ b/solution.py
@@ -47,7 +47,7 @@
     local_proj = lax.dot_general(
         eigvecs, pulled, (((0,), (0,)), ((), ())), precision=lax.Precision.HIGHEST
     )
-    projected = lax.psum(local_proj, ("narrow", "nys"))
+    projected = lax.psum(lax.psum(local_proj, "narrow"), "nys")
     scaled_proj = corrections[:, None] * projected
     gradient = jnp.dot(k_batch, residual, preferred_element_type=jnp.float32)
     corrected = jnp.dot(eigvecs, scaled_proj, precision=lax.Precision.HIGHEST).astype(jnp.bfloat16)

time: 1290 us -> 1070 us (0.83)
  waiting for transfers between devices: 1140 us -> 921 us
    psum x1 -> x2, waiting for transfers between devices: 301 us -> 132 us  [per_device(): projected = lax.psum(lax.psum(local_proj, 'narrow'), 'nys')]
    all_gather x1, waiting for transfers between devices: 158 us -> 106 us  [per_device(): lax.all_gather(nystrom_points, ('narrow', 'nys'), axis=0, tiled=True)]
  transfers between devices with their start and end apart: 4 -> 5, of which waited for: 4 -> 5; matrix products, arithmetic and copies ran while one was open for 1% -> 1% of each run, Pallas kernels for 0% -> 0%
where the time goes in v1:
time: 1070 us
  waiting for transfers between devices  921 us (86%)
  blocking collectives  81.6 us (8%)
  matrix products  33.3 us (3%)
  between operations  14.7 us (1%)
    all_gather x1, waiting for transfers between devices, per_device(): lax.all_gather(batch_points, ('narrow', 'wide', 'nys'), axis=0, tiled=True)  524 us
    all_gather x1, waiting for transfers between devices, per_device(): coefs = lax.all_gather(corrected, ('narrow', 'nys'), axis=0, tiled=True)  158 us
    psum x2, waiting for transfers between devices, per_device(): projected = lax.psum(lax.psum(local_proj, 'narrow'), 'nys')  132 us
    all_gather x1, waiting for transfers between devices, per_device(): lax.all_gather(nystrom_points, ('narrow', 'nys'), axis=0, tiled=True)  106 us
    psum x1, blocking collectives, per_device(): lax.psum(partial_value - placed, ('narrow', 'wide', 'nys'))  81.6 us
  transfers between devices with their start and end apart: 5, of which 5 were waited for; matrix products, arithmetic and copies ran while one was open for 1% of the time, Pallas kernels for 0%

profile of v1, /device:TPU:2, one launch (start us, length us, event | category | flops | bytes accessed | tf_op | source)
XLA Modules:
  0.0 1067.8 jit_solution(1380728799374887871)
XLA Ops:
  7.4 0.0 copy-start
  7.4 0.0 all-gather.9.cloned.1.call-start
  7.4 0.7 all-gather.9.cloned.1.call-update
  8.1 0.0 all-reduce.4.cloned.1.call-start
  8.1 0.9 copy.9
  9.1 0.2 broadcast_in_dim.2
  9.3 6.3 dynamic_update_slice.3
  15.6 1.0 multiply_reduce_fusion.3
  16.7 2.1 multiply_reduce_fusion.1
  18.7 523.6 %all-gather.9.cloned.1.call-done = bf16[256,2,1024]{2,1,0:T(2,128)(2,1)} async-done(((bf16[1,2,1024]{2,1,0:T(2,128)(2,1)}), bf16[256,2,1024]{2,1,0:T(2,128)(2,1)}) %all-gather.9.cloned.1.call-update) | async-done | bytes 1048592 | tf_op jit(solution)/shard_map/all_gather | solution.py:27
  542.3 1.5 reshape.6
  543.8 0.3 multiply_reduce_fusion.2
  544.1 0.0 copy-start.1
  544.1 3.8 exponential_convert_fusion.1
  547.9 0.0 copy-start.2
  547.9 1.1 copy-done.2
  549.0 0.0 copy-done.1
  549.0 0.0 copy-start.4
  549.0 2.6 multiply_subtract_fusion.1
  551.6 0.0 copy-start.5
  551.6 81.6 %all-reduce.7 = bf16[512,1000]{0,1:T(8,128)(2,1)S(1)} all-reduce(f32[512,1000]{0,1:T(8,128)} %multiply_subtract_fusion.1), channel_id=1, replica_groups=mesh['narrow'=8,'wide'=8,'nys'=4] {'narrow','wide','nys'}, use_global_device_ids=true, to_apply=%region_2.0 | all-reduce | flops 512000 | bytes 3072000 | tf_op jit(solution)/shard_map/psum | solution.py:44
  633.1 0.0 copy-done.4
  633.1 0.8 fusion.12
  634.0 0.0 copy-done
  634.0 1.6 convolution_bitcast_fusion
  635.5 0.0 all-reduce.4.cloned.1.call-update
  635.6 0.0 all-reduce.6.cloned.1.call-start
  635.6 80.1 %all-reduce.4.cloned.1.call-done = f32[160,1000]{1,0:T(8,128)} async-done(((f32[160,1000]{1,0:T(8,128)}), f32[160,1000]{1,0:T(8,128)}) %all-reduce.4.cloned.1.call-update) | async-done | bytes 640016 | tf_op jit(solution)/shard_map/psum | solution.py:50
  715.7 0.0 all-reduce.6.cloned.1.call-update
  715.7 0.0 all-gather.5.cloned.1.call-start
  715.8 0.5 all-gather.5.cloned.1.call-update
  716.3 0.2 all-gather.7.cloned.1.call-start
  716.5 52.4 %all-reduce.6.cloned.1.call-done = f32[160,1000]{1,0:T(8,128)} async-done(((f32[160,1000]{1,0:T(8,128)}), f32[160,1000]{1,0:T(8,128)}) %all-reduce.6.cloned.1.call-update) | async-done | bytes 640016 | tf_op jit(solution)/shard_map/psum | solution.py:50
  768.9 0.0 copy-done.5
  768.9 2.3 fusion.4
  771.2 0.0 all-gather.7.cloned.1.call-update
  771.3 105.7 %all-gather.5.cloned.1.call-done = bf16[2048,1024]{1,0:T(8,128)(2,1)} async-done(((bf16[64,1024]{1,0:T(8,128)(2,1)}), bf16[2048,1024]{1,0:T(8,128)(2,1)}) %all-gather.5.cloned.1.call-update) | async-done | bytes 4194320 | tf_op jit(solution)/shard_map/all_gather | solution.py:54
  876.9 3.1 multiply_reduce_fusion
  880.0 0.0 copy-start.3
  880.0 158.5 %all-gather.7.cloned.1.call-done = bf16[2048,1000]{1,0:T(8,128)(2,1)} async-done(((bf16[64,1000]{1,0:T(8,128)(2,1)}), bf16[2048,1000]{1,0:T(8,128)(2,1)}) %all-gather.7.cloned.1.call-update) | async-done | bytes 4096016 | tf_op jit(solution)/shard_map/all_gather | solution.py:55
  1038.5 15.5 %fusion.13 = f32[1024,1000]{0,1:T(8,128)} fusion(bf16[2048,1000]{1,0:T(8,128)(2,1)} %all-gather.7.cloned.1.call-done, bf16[1024,1024]{1,0:T(8,128)(2,1)} %param.7, bf16[2048,1024]{1,0:T(8,128)(2,1)} %all-gather.5.cloned.1.call-done, f32[2048]{0:T(1024)S(1)} %multiply_reduce_fusion, f32[1024]{0:T(1024)S(1)} %multiply_reduce_fusion.1), kind=kOutput, calls=%fused_computation.21 | convolution fusion | flops 8503951360 | bytes 14495744 | tf_op jit(solution)/shard_map/dot_general | solution.py:57
  1054.0 0.0 copy-done.3
  1054.0 6.7 multiply_subtract_fusion
Async XLA Ops:
  7.4 626.6 %copy-start = (f32[64,160]{1,0:T(8,128)S(1)}, f32[64,160]{1,0:T(8,128)}, u32[]{:S(2)}) copy-start(f32[64,160]{1,0:T(8,128)} %param.12) | copy-start | bytes 122884
  7.4 535.0 %all-gather.9.cloned.1.call-start = ((), (), s32[]{:S(2)}) async-start(), calls=%async_computation.4 | async-start | bytes 1052672 | tf_op jit(solution)/shard_map/all_gather | solution.py:27
  8.1 707.6 %all-reduce.4.cloned.1.call-start = ((), (), s32[]{:S(2)}) async-start(), calls=%async_computation.1 | async-start | bytes 1310720 | tf_op jit(solution)/shard_map/psum | solution.py:50
  544.1 4.9 copy-start.1
  547.9 1.1 copy-start.2
  549.0 84.1 %copy-start.4 = (bf16[64,1024]{1,0:T(8,128)(2,1)S(1)}, bf16[64,1024]{1,0:T(8,128)(2,1)}, u32[]{:S(2)}) copy-start(bf16[64,1024]{1,0:T(8,128)(2,1)} %param.11) | copy-start | bytes 393220
  551.6 217.3 %copy-start.5 = (f32[160]{0:T(256)S(1)}, f32[160]{0:T(256)}, u32[]{:S(2)}) copy-start(f32[160]{0:T(256)} %param.13) | copy-start | bytes 1924
  635.6 133.3 %all-reduce.6.cloned.1.call-start = ((), (), s32[]{:S(2)}) async-start(), calls=%async_computation.2 | async-start | bytes 1310720 | tf_op jit(solution)/shard_map/psum | solution.py:50
  715.7 161.2 %all-gather.5.cloned.1.call-start = ((), (), s32[]{:S(2)}) async-start(), calls=%async_computation | async-start | bytes 4325376 | tf_op jit(solution)/shard_map/all_gather | solution.py:54
  716.3 322.2 %all-gather.7.cloned.1.call-start = ((), (), s32[]{:S(2)}) async-start(), calls=%async_computation.3 | async-start | bytes 4325376 | tf_op jit(solution)/shard_map/all_gather | solution.py:55
  880.0 174.0 %copy-start.3 = (bf16[1024,512]{1,0:T(8,128)(2,1)S(1)}, bf16[1024,512]{1,0:T(8,128)(2,1)}, u32[]{:S(2)}) copy-start(bf16[1024,512]{1,0:T(8,128)(2,1)} %copy-done.2) | copy-start | bytes 3145732
Sparse Core Ops, SparseCore 0:
  10.0 532.3 all-gather.8
  635.7 79.9 all-reduce.3
  718.0 50.8 all-reduce.5
Sparse Core Ops, SparseCore 1:
  718.0 158.9 all-gather.4
  878.6 159.9 all-gather.6

commit v2 on v0

--- a/solution.py
+++ b/solution.py
@@ -51,8 +51,16 @@
     scaled_proj = corrections[:, None] * projected
     gradient = jnp.dot(k_batch, residual, preferred_element_type=jnp.float32)
     corrected = jnp.dot(eigvecs, scaled_proj, precision=lax.Precision.HIGHEST).astype(jnp.bfloat16)
-    points = lax.all_gather(nystrom_points, ("narrow", "nys"), axis=0, tiled=True)
-    coefs = lax.all_gather(corrected, ("narrow", "nys"), axis=0, tiled=True)
+    points, coefs = jnp.split(
+        lax.all_gather(
+            jnp.concatenate([nystrom_points, corrected], axis=1),
+            ("narrow", "nys"),
+            axis=0,
+            tiled=True,
+        ),
+        [nystrom_points.shape[1]],
+        axis=1,
+    )
     tile = kernel_with(centers, center_sq, points)
     nystrom_term = jnp.dot(tile, coefs, preferred_element_type=jnp.float32)
     return weights - RATE / BATCH * (gradient - nystrom_term)

time: 1290 us -> 1140 us (0.88)
  waiting for transfers between devices: 1140 us -> 996 us
    all_gather x2 -> x1, waiting for transfers between devices: 315 us -> 169 us  [per_device(): lax.all_gather(jnp.concatenate([nystrom_points, corrected], axis=1), ('na...]
  transfers between devices with their start and end apart: 4 -> 3, of which waited for: 4 -> 3; matrix products, arithmetic and copies ran while one was open for 1% -> 1% of each run, Pallas kernels for 0% -> 0%
where the time goes in v2:
time: 1140 us
  waiting for transfers between devices  996 us (87%)
  blocking collectives  81.6 us (7%)
  matrix products  32.6 us (3%)
  between operations  13.2 us (1%)
    all_gather x1, waiting for transfers between devices, per_device(): lax.all_gather(batch_points, ('narrow', 'wide', 'nys'), axis=0, tiled=True)  524 us
    psum x1, waiting for transfers between devices, per_device(): projected = lax.psum(local_proj, ('narrow', 'nys'))  302 us
    all_gather x1, waiting for transfers between devices, per_device(): lax.all_gather(jnp.concatenate([nystrom_points, corrected], axis=1), ('na...  169 us
    psum x1, blocking collectives, per_device(): lax.psum(partial_value - placed, ('narrow', 'wide', 'nys'))  81.6 us
  transfers between devices with their start and end apart: 3, of which 3 were waited for; matrix products, arithmetic and copies ran while one was open for 1% of the time, Pallas kernels for 0%

profile of v2, /device:TPU:2, one launch (start us, length us, event | category | flops | bytes accessed | tf_op | source)
XLA Modules:
  0.0 1140.5 jit_solution(4068086824592146472)
XLA Ops:
  6.5 0.0 copy-start
  6.5 0.0 all-gather.6.cloned.1.call-start
  6.5 0.7 all-gather.6.cloned.1.call-update
  7.3 0.0 all-reduce.3.cloned.1.call-start
  7.3 0.9 copy.9
  8.2 0.2 broadcast_in_dim.2
  8.5 6.3 dynamic_update_slice.3
  14.8 1.0 multiply_reduce_fusion.3
  15.8 2.1 multiply_reduce_fusion.1
  17.9 523.6 %all-gather.6.cloned.1.call-done = bf16[256,2,1024]{2,1,0:T(2,128)(2,1)} async-done(((bf16[1,2,1024]{2,1,0:T(2,128)(2,1)}), bf16[256,2,1024]{2,1,0:T(2,128)(2,1)}) %all-gather.6.cloned.1.call-update) | async-done | bytes 1048592 | tf_op jit(solution)/shard_map/all_gather | solution.py:27
  541.5 1.5 reshape.6
  543.0 0.3 multiply_reduce_fusion.2
  543.3 0.0 copy-start.1
  543.3 3.8 exponential_convert_fusion
  547.1 0.0 copy-start.2
  547.1 1.1 copy-done.2
  548.2 0.0 copy-done.1
  548.2 0.0 copy-start.4
  548.2 2.6 multiply_subtract_fusion.1
  550.7 0.0 copy-start.5
  550.7 81.6 %all-reduce.4 = bf16[512,1000]{0,1:T(8,128)(2,1)S(1)} all-reduce(f32[512,1000]{0,1:T(8,128)} %multiply_subtract_fusion.1), channel_id=1, replica_groups=mesh['narrow'=8,'wide'=8,'nys'=4] {'narrow','wide','nys'}, use_global_device_ids=true, to_apply=%region_2.0 | all-reduce | flops 512000 | bytes 3072000 | tf_op jit(solution)/shard_map/psum | solution.py:44
  632.3 0.0 copy-done.4
  632.3 0.8 fusion.23
  633.2 0.0 copy-done
  633.2 1.6 convolution_bitcast_fusion
  634.7 0.0 all-reduce.3.cloned.1.call-update
  634.7 0.2 all-gather.4.cloned.1.call-start
  635.0 302.3 %all-reduce.3.cloned.1.call-done = f32[160,1000]{1,0:T(8,128)} async-done(((f32[160,1000]{1,0:T(8,128)}), f32[160,1000]{1,0:T(8,128)}) %all-reduce.3.cloned.1.call-update) | async-done | bytes 640016 | tf_op jit(solution)/shard_map/psum | solution.py:50
  937.3 0.0 copy-done.5
  937.3 1.7 fusion.15
  939.0 0.7 pad_maximum_fusion
  939.7 0.0 all-gather.4.cloned.1.call-update
  939.8 169.0 %all-gather.4.cloned.1.call-done = bf16[2048,2024]{1,0:T(8,128)(2,1)} async-done(((bf16[64,2024]{1,0:T(8,128)(2,1)}), bf16[2048,2024]{1,0:T(8,128)(2,1)}) %all-gather.4.cloned.1.call-update) | async-done | bytes 8290320 | tf_op jit(solution)/shard_map/all_gather | solution.py:55
  1108.7 3.1 multiply_reduce_fusion
  1111.8 0.0 copy-start.3
  1111.8 15.5 %fusion.6 = f32[1024,1000]{0,1:T(8,128)} fusion(bf16[2048,2024]{1,0:T(8,128)(2,1)} %all-gather.4.cloned.1.call-done, bf16[1024,1024]{1,0:T(8,128)(2,1)} %param.7, f32[2048]{0:T(1024)S(1)} %multiply_reduce_fusion, f32[1024]{0:T(1024)S(1)} %multiply_reduce_fusion.1), kind=kOutput, calls=%fused_computation.8 | convolution fusion | flops 8503951360 | bytes 14495744 | tf_op jit(solution)/shard_map/dot_general | solution.py:65
  1127.3 0.0 copy-done.3
  1127.4 6.7 multiply_subtract_fusion
Async XLA Ops:
  6.5 626.6 %copy-start = (f32[64,160]{1,0:T(8,128)S(1)}, f32[64,160]{1,0:T(8,128)}, u32[]{:S(2)}) copy-start(f32[64,160]{1,0:T(8,128)} %param.12) | copy-start | bytes 122884
  6.5 535.0 %all-gather.6.cloned.1.call-start = ((), (), s32[]{:S(2)}) async-start(), calls=%async_computation.2 | async-start | bytes 1052672 | tf_op jit(solution)/shard_map/all_gather | solution.py:27
  7.3 930.1 %all-reduce.3.cloned.1.call-start = ((), (), s32[]{:S(2)}) async-start(), calls=%async_computation | async-start | bytes 1310720 | tf_op jit(solution)/shard_map/psum | solution.py:50
  543.3 4.9 copy-start.1
  547.1 1.1 copy-start.2
  548.2 84.1 %copy-start.4 = (bf16[64,1024]{1,0:T(8,128)(2,1)S(1)}, bf16[64,1024]{1,0:T(8,128)(2,1)}, u32[]{:S(2)}) copy-start(bf16[64,1024]{1,0:T(8,128)(2,1)} %param.11) | copy-start | bytes 393220
  550.7 386.6 %copy-start.5 = (f32[160]{0:T(256)S(1)}, f32[160]{0:T(256)}, u32[]{:S(2)}) copy-start(f32[160]{0:T(256)} %param.13) | copy-start | bytes 1924
  634.7 474.0 %all-gather.4.cloned.1.call-start = ((), (), s32[]{:S(2)}) async-start(), calls=%async_computation.1 | async-start | bytes 8650752 | tf_op jit(solution)/shard_map/all_gather | solution.py:55
  1111.8 15.6 %copy-start.3 = (bf16[1024,512]{1,0:T(8,128)(2,1)S(1)}, bf16[1024,512]{1,0:T(8,128)(2,1)}, u32[]{:S(2)}) copy-start(bf16[1024,512]{1,0:T(8,128)(2,1)} %copy-done.2) | copy-start | bytes 3145732
Sparse Core Ops, SparseCore 0:
  9.2 532.3 all-gather.5
  634.9 302.4 all-reduce.2
  939.9 168.8 all-gather.3
